TPU v7x, 32 devices: a whole 2x2x4 slice. The times are simulated.
32 devices in a mesh: groups: 2 (over x), lon: 16 (over z, y, core).
Axes of the slice: x: 2, y: 2, z: 4, core: 2. Of those that a mesh axis runs over, the one named last changes fastest.
Arguments:
- fields: bfloat16 [32, 32, 1500], P(('groups', 'lon')), parts along dimension 0, may hold values from -6 to 6
- level_ids: int32 [6], P('groups'), parts along dimension 0, may hold values from 0 to 2, each once
- embed_weight: bfloat16 [500, 512], replicated, may hold values from -0.25 to 0.25
- level_embed: bfloat16 [3, 512], replicated, may hold values from -6 to 6
- enc_gain: float32 [512], replicated, may hold values from 0.1 to 1.9
- latent_query: bfloat16 [2, 512], replicated, may hold values from -0.049804688 to 0.049804688
- kv_weight: bfloat16 [512, 1024], replicated, may hold values from -0.25 to 0.25
- pool_out: bfloat16 [512, 512], replicated, may hold values from -0.25 to 0.25
- attn_gain: float32 [512], replicated, may hold values from 0.1 to 1.9
- qkv_weight: bfloat16 [512, 1536], replicated, may hold values from -0.25 to 0.25
- attn_proj: bfloat16 [512, 512], replicated, may hold values from -0.25 to 0.25
- mlp_gain: float32 [512], replicated, may hold values from 0.1 to 1.9
- mlp_up: bfloat16 [512, 2048], replicated, may hold values from -0.25 to 0.25
- mlp_down: bfloat16 [2048, 512], replicated, may hold values from -0.125 to 0.125
- level_mix: float32 [3, 2], replicated, may hold values from 0.25 to 4
- dec_gain: float32 [512], replicated, may hold values from 0.1 to 1.9
- dec_weight: bfloat16 [512, 500], replicated, may hold values from -0.25 to 0.25
Outputs:
- forecast: bfloat16 [32, 32, 1500], P(('groups', 'lon')), parts along dimension 0
There are 2 independent parts, one for each index of `groups`. A program takes and returns all parts, laid end to end along the dimension named above; an argument that names none is the same for every part. Nothing has to cross between parts.
Inputs may be any that keep to these rules, and one draw needn't show every extreme that they name: level_ids holds each of 0 to 2 once.
All inputs are finite; a program needn't handle non-finite values.
Results may differ from a plain program's by a relative error of at most 0.014.
Values may be sent and summed in bfloat16 or wider, within the bound.
A program may use at most 128 MiB of HBM per device.

v0:
```python
import jax
import jax.numpy as jnp
from jax import lax
from jax.sharding import PartitionSpec as P

D = 512
HEADS = 8
PIN = 500
LEV = 3
LATL = 2
W_LAT = 4
W_LON = 8
STEPS = 2
ROW_PARTS = 4


norm_eps = 1e-05
head_eps = 1e-06


def product(einsum_form, left_side, right_side):
    return jnp.einsum(einsum_form, left_side, right_side, preferred_element_type=jnp.float32)


def layer_norm(values, scale_row):
    average = jnp.mean(values, axis=-1, keepdims=True)
    centred = values - average
    spread = jnp.mean(centred * centred, axis=-1, keepdims=True)
    return centred * lax.rsqrt(spread + norm_eps) * scale_row


def unit_heads(values):
    shaped = values.reshape(values.shape[:-1] + (HEADS, D // HEADS))
    mean_square = jnp.mean(shaped * shaped, axis=-1, keepdims=True)
    return (shaped * lax.rsqrt(mean_square + head_eps)).reshape(values.shape)


def level_tables(level_ids, level_embed, level_mix):
    picker = (level_ids[:, None] == jnp.arange(LEV, dtype=jnp.int32)[None, :]).astype(jnp.float32)
    embeds = jnp.dot(picker, level_embed.astype(jnp.float32), precision=lax.Precision.HIGHEST)
    mixing = jnp.dot(picker, level_mix, precision=lax.Precision.HIGHEST)
    return (embeds, mixing)


def head_tables(queries):
    head_dim = D // HEADS
    feature_head = jnp.arange(D, dtype=jnp.int32) // head_dim
    head_ids = jnp.arange(HEADS, dtype=jnp.int32)
    spreader = (head_ids[:, None] == feature_head[None, :]).astype(jnp.bfloat16)
    on_head = (feature_head[:, None] == head_ids[None, :]).astype(jnp.bfloat16)
    query_table = (queries.T[:, :, None] * on_head[:, None, :]).reshape(D, LATL * HEADS)
    return (query_table, spreader)


def encode(
    flat_fields,
    embeds,
    query_table,
    spreader,
    embed_weight,
    enc_gain,
    kv_weight,
    pool_out,
    latent_query,
):
    head_dim = D // HEADS
    patch_count = flat_fields.shape[0]
    patches = flat_fields.reshape(patch_count * LEV, PIN)
    tokens = jnp.dot(patches, embed_weight, preferred_element_type=jnp.float32).reshape(
        patch_count, LEV, D
    )
    tokens = layer_norm(tokens + embeds[None], enc_gain).astype(jnp.bfloat16)
    keyval = jnp.dot(
        tokens.reshape(patch_count * LEV, D), kv_weight, preferred_element_type=jnp.float32
    )
    key_rows = unit_heads(keyval[:, :D]).astype(jnp.bfloat16)
    value_rows = keyval[:, D:].astype(jnp.bfloat16).reshape(patch_count, LEV, 1, D)
    scores = jnp.dot(key_rows, query_table, preferred_element_type=jnp.float32) * head_dim ** (-0.5)
    scores = scores.reshape(patch_count, LEV, LATL * HEADS)
    weights = jnp.exp(scores)
    weights = (weights / jnp.sum(weights, axis=1, keepdims=True)).astype(jnp.bfloat16)
    spread_weights = jnp.dot(
        weights.reshape(patch_count * LEV * LATL, HEADS),
        spreader,
        preferred_element_type=jnp.float32,
    )
    spread_weights = spread_weights.reshape(patch_count, LEV, LATL, D)
    pooled = jnp.sum(spread_weights * value_rows.astype(jnp.float32), axis=1)
    pooled = pooled.astype(jnp.bfloat16).reshape(patch_count * LATL, D)
    latents = jnp.dot(pooled, pool_out, preferred_element_type=jnp.float32).reshape(
        patch_count, LATL, D
    )
    return (latents + latent_query.astype(jnp.float32)[None]).astype(jnp.bfloat16)


def increments(backbone_out, embeds, mixing, dec_gain, dec_weight):
    patch_count = backbone_out.shape[0]
    blended = mixing[None, :, 0, None] * backbone_out[:, None, 0, :].astype(jnp.float32)
    blended = blended + mixing[None, :, 1, None] * backbone_out[:, None, 1, :].astype(jnp.float32)
    blended = blended + embeds[None]
    normed = layer_norm(blended, dec_gain).astype(jnp.bfloat16)
    result = jnp.dot(
        normed.reshape(patch_count * LEV, D), dec_weight, preferred_element_type=jnp.float32
    )
    return result.astype(jnp.bfloat16).reshape(patch_count, LEV * PIN)


def window_block(shifted, attn_gain, qkv_weight, attn_proj):
    head_dim = D // HEADS
    lat_count, lon_count = (shifted.shape[0], shifted.shape[1])
    lat_win, lon_win = (lat_count // W_LAT, lon_count // W_LON)
    inside = W_LAT * W_LON * LATL
    flat_tokens = shifted.reshape(-1, D)
    normed = layer_norm(flat_tokens.astype(jnp.float32), attn_gain).astype(jnp.bfloat16)
    projected = jnp.dot(normed, qkv_weight, preferred_element_type=jnp.float32)
    query_heads = unit_heads(projected[:, :D]).astype(jnp.bfloat16)
    key_heads = unit_heads(projected[:, D : 2 * D]).astype(jnp.bfloat16)
    value_heads = projected[:, 2 * D :].astype(jnp.bfloat16)

    def to_windows(head_data):
        shaped = head_data.reshape(lat_win, W_LAT, lon_win, W_LON, LATL, HEADS, head_dim)
        return shaped.transpose(0, 2, 5, 1, 3, 4, 6).reshape(
            lat_win, lon_win, HEADS, inside, head_dim
        )

    scores = product(
        "abhqc,abhkc->abhqk", to_windows(query_heads), to_windows(key_heads)
    ) * head_dim ** (-0.5)
    row_index = jnp.arange(lat_count, dtype=jnp.int32).reshape(lat_win, W_LAT)
    region = (row_index >= lat_count - W_LAT // 2).astype(jnp.int32)
    region_tok = jnp.broadcast_to(region[:, :, None, None], (lat_win, W_LAT, W_LON, LATL)).reshape(
        lat_win, inside
    )
    allowed = (region_tok[:, :, None] == region_tok[:, None, :]).astype(jnp.float32)
    weights = jnp.exp(scores) * allowed[:, None, None, :, :]
    weights = (weights / jnp.sum(weights, axis=-1, keepdims=True)).astype(jnp.bfloat16)
    win_mix = product("abhqk,abhkc->abhqc", weights, to_windows(value_heads)).astype(jnp.bfloat16)
    win_mix = win_mix.reshape(lat_win, lon_win, HEADS, W_LAT, W_LON, LATL, head_dim)
    win_mix = win_mix.transpose(0, 3, 1, 4, 5, 2, 6).reshape(-1, D)
    attended = flat_tokens.astype(jnp.float32) + jnp.dot(
        win_mix, attn_proj, preferred_element_type=jnp.float32
    )
    return attended.astype(jnp.bfloat16).reshape(shifted.shape)


def mlp_block(restored, mlp_gain, mlp_up, mlp_down):
    flat_tokens = restored.reshape(-1, D)
    normed = layer_norm(flat_tokens.astype(jnp.float32), mlp_gain).astype(jnp.bfloat16)
    hidden = jax.nn.gelu(jnp.dot(normed, mlp_up, preferred_element_type=jnp.float32)).astype(
        jnp.bfloat16
    )
    result = flat_tokens.astype(jnp.float32) + jnp.dot(
        hidden, mlp_down, preferred_element_type=jnp.float32
    )
    return result.astype(jnp.bfloat16).reshape(restored.shape)


def shards(
    fields,
    level_ids,
    embed_weight,
    level_embed,
    enc_gain,
    latent_query,
    kv_weight,
    pool_out,
    attn_gain,
    qkv_weight,
    attn_proj,
    mlp_gain,
    mlp_up,
    mlp_down,
    level_mix,
    dec_gain,
    dec_weight,
):
    embeds, mixing = level_tables(level_ids, level_embed, level_mix)
    queries = unit_heads(latent_query.astype(jnp.float32)).astype(jnp.bfloat16)
    query_table, spreader = head_tables(queries)
    field_width = fields.shape[2]
    local_count = fields.shape[1]
    devices = lax.axis_size("lon")
    piece_cols = local_count // devices
    lat_count = devices // ROW_PARTS
    lon_dev = piece_cols * ROW_PARTS
    half_cols = W_LON // 2
    lag = half_cols // piece_cols
    piece = lax.axis_index("lon") // lat_count
    carry = (piece - lag) // ROW_PARTS
    latent_width = LATL * D
    current = fields
    for turn_index in range(STEPS):
        latents = encode(
            current.reshape(local_count, field_width),
            embeds,
            query_table,
            spreader,
            embed_weight,
            enc_gain,
            kv_weight,
            pool_out,
            latent_query,
        )
        blocks = latents.reshape(devices, piece_cols, latent_width)
        blocks = jnp.roll(blocks, carry, axis=0)
        got = lax.all_to_all(
            blocks.reshape(1, local_count, latent_width),
            "lon",
            split_axis=1,
            concat_axis=0,
            tiled=True,
        )
        tiles = got.reshape(ROW_PARTS, lat_count, piece_cols, latent_width).transpose(1, 0, 2, 3)
        tiles = jnp.roll(tiles, -lag, axis=1).reshape(lat_count, lon_dev, latent_width)
        tiles = jnp.roll(tiles, -(W_LAT // 2), axis=0).reshape(lat_count, lon_dev, LATL, D)
        attended = window_block(tiles, attn_gain, qkv_weight, attn_proj)
        backbone_out = mlp_block(attended, mlp_gain, mlp_up, mlp_down)
        values = backbone_out.reshape(lat_count, lon_dev, latent_width)
        extent = values.shape[2]
        values = jnp.roll(values, W_LAT // 2, axis=0)
        values = jnp.roll(values.reshape(lat_count, ROW_PARTS, piece_cols, extent), lag, axis=1)
        outgoing = values.transpose(1, 0, 2, 3).reshape(devices, piece_cols, extent)
        received = lax.all_to_all(outgoing, "lon", split_axis=0, concat_axis=1, tiled=True)
        home = received.reshape(devices, piece_cols, received.shape[2])
        home = jnp.roll(home, -carry, axis=0)
        home_latents = home.reshape(local_count, received.shape[2])
        added = increments(
            home_latents.reshape(local_count, LATL, D), embeds, mixing, dec_gain, dec_weight
        )
        added = added.reshape(current.shape)
        current = (current.astype(jnp.float32) + added.astype(jnp.float32)).astype(jnp.bfloat16)
    return current


def solution(mesh):
    placed = (
        P(("groups", "lon"), None, None),
        P("groups"),
        P(),
        P(),
        P(),
        P(),
        P(),
        P(),
        P(),
        P(),
        P(),
        P(),
        P(),
        P(),
        P(),
        P(),
        P(),
    )
    return jax.shard_map(
        shards,
        mesh=mesh,
        in_specs=placed,
        out_specs=P(("groups", "lon"), None, None),
        check_vma=False,
    )
```

profile of v0, /device:TPU:0, one launch (start us, length us, event | category | flops | bytes accessed | tf_op | source)
XLA Modules:
  0.0 169.1 jit_solution(9471271311963540494)
XLA Ops:
  0.6 1.1 dot_general.83
  2.5 1.3 fusion.138
  5.7 1.2 fusion.142
  7.6 1.8 %copy.290 = f32[96,512]{0,1:T(8,128)} copy(f32[96,512]{1,0:T(8,128)} %slice_multiply_fusion.1) | data formatting | bytes 393216 | tf_op jit(solution)/shard_map/mul | solution.py:34
  9.3 1.0 bitcast_reduce_fusion.1
  11.0 1.8 %copy.291 = f32[96,512]{1,0:T(8,128)} copy(f32[96,512]{0,1:T(8,128)} %bitcast.127) | data formatting | bytes 393216 | tf_op jit(solution)/shard_map/mul | solution.py:35
  13.5 1.3 convert_multiply_fusion
  14.8 1.4 mul.475
  16.1 1.4 reduce_sum.264
  18.8 1.4 mul.477
  21.5 1.7 fusion.17
  23.1 1.4 copy.292
  24.6 1.4 exp.32
  26.0 1.6 exp.31
  30.0 1.0 reshape.615
  31.1 0.9 divide_convert_fusion.5
  32.9 1.2 fusion.8
  35.1 1.0 reduce.8
  36.7 7.4 %all-to-all-start = ((bf16[16,2,1024]{2,1,0:T(2,128)(2,1)}), bf16[16,2,1024]{2,1,0:T(2,128)(2,1)}, u32[]{:S(2)}, u32[]{:S(2)}) async-start(bf16[16,2,1024]{2,1,0:T(2,128)(2,1)} %reshape.632), calls=%async_computation | async-start | bytes 131072 | tf_op jit(solution)/shard_map/all_to_all | solution.py:206
  45.2 1.0 add.248
  47.0 4.1 %all-to-all-done = bf16[16,2,1024]{2,1,0:T(2,128)(2,1)} async-done(((bf16[16,2,1024]{2,1,0:T(2,128)(2,1)}), bf16[16,2,1024]{2,1,0:T(2,128)(2,1)}, u32[]{:S(2)}, u32[]{:S(2)}) %all-to-all-start) | async-done | bytes 65568 | tf_op jit(solution)/shard_map/all_to_all | solution.py:206
  52.0 1.0 bitcast_reduce_fusion.3
  54.8 0.9 reshape.616
  56.0 1.9 %fusion.72 = f32[64,1536]{1,0:T(8,128)S(1)} fusion(bf16[512,1536]{1,0:T(8,128)(2,1)} %param.28, f32[64,512]{1,0:T(8,128)S(1)} %reshape.616, f32[512]{0:T(512)} %param.27, f32[64]{0:T(128)S(1)} %add_rsqrt_fusion.14, f32[64]{0:T(128)S(1)} %broadcast_multiply_fusion.7), kind=kOutput, calls=%fused_computation.140 | convolution fusion | flops 100794368 | bytes 2099712 | tf_op jit(solution)/shard_map/dot_general | solution.py:115
  59.4 1.7 %mul.492 = f32[64,8,64]{2,1,0:T(8,128)} reshape(f32[64,512]{1,0:T(8,128)} %get-tuple-element.13) | data formatting | bytes 262144 | tf_op jit(solution)/shard_map/mul | solution.py:34
  61.1 1.1 reduce_sum.269
  62.8 1.3 add_rsqrt_fusion.4
  65.7 1.7 %mul.494 = f32[64,512]{1,0:T(8,128)} reshape(f32[64,8,64]{2,1,0:T(8,128)} %mul.493) | data formatting | bytes 262144 | tf_op jit(solution)/shard_map/mul | solution.py:35
  67.4 1.7 %mul.497 = f32[64,8,64]{2,1,0:T(8,128)} reshape(f32[64,512]{1,0:T(8,128)} %get-tuple-element.12) | data formatting | bytes 262144 | tf_op jit(solution)/shard_map/mul | solution.py:34
  69.1 1.1 reduce_sum.270
  70.8 1.3 add_rsqrt_fusion.3
  73.7 1.7 %mul.499 = f32[64,512]{1,0:T(8,128)} reshape(f32[64,8,64]{2,1,0:T(8,128)} %mul.498) | data formatting | bytes 262144 | tf_op jit(solution)/shard_map/mul | solution.py:35
  75.4 1.8 %multiply_convert_fusion.11 = (bf16[64,512]{1,0:T(8,128)(2,1)}, bf16[64,512]{1,0:T(8,128)(2,1)}) fusion(f32[64,512]{1,0:T(8,128)} %mul.499, f32[64,1536]{1,0:T(8,128)} %copy-done.2, f32[64,512]{1,0:T(8,128)} %mul.494), kind=kLoop, calls=%fused_computation.112 | loop fusion | flops 131072 | bytes 655360 | tf_op jit(solution)/shard_map/convert_element_type | solution.py:117
  77.2 1.6 reshape.593
  78.8 1.7 copy.306
  80.5 1.6 reshape.595
  82.1 1.7 copy.309
  83.8 1.6 reshape.597
  85.4 1.7 copy.310
  87.0 1.9 %fusion.5 = f32[8,64,64]{1,2,0:T(8,128)} fusion(bf16[8,64,64]{2,1,0:T(8,128)(2,1)} %bitcast.136, bf16[8,64,64]{2,1,0:T(8,128)(2,1)} %bitcast.138, f32[64,64]{0,1:T(8,128)S(1)} %compare_convert_fusion), kind=kOutput, calls=%fused_computation.9 | convolution fusion | flops 4259840 | bytes 278528 | tf_op jit(solution)/shard_map/abhqc,abhkc->abhqk/dot_general | solution.py:22
  88.9 2.0 %convolution_convert_fusion.1 = bf16[8,64,64]{2,1,0:T(8,128)(2,1)} fusion(bf16[8,64,64]{2,1,0:T(8,128)(2,1)} %bitcast.153, f32[8,64,64]{1,2,0:T(8,128)} %fusion.5), kind=kOutput, calls=%fused_computation.13 | convolution fusion | flops 4293183 | bytes 262144 | tf_op jit(solution)/shard_map/abhqk,abhkc->abhqc/dot_general | solution.py:22
  90.9 1.7 %copy.396 = bf16[1,1,8,4,8,2,64]{6,2,5,4,3,1,0:T(8,128)(2,1)} copy(bf16[1,1,8,4,8,2,64]{6,5,4,3,2,1,0:T(2,128)(2,1)} %bitcast.154) | data formatting | bytes 131072 | tf_op jit(solution)/shard_map/reshape | solution.py:138
  92.6 1.1 reshape.600
  93.6 1.4 fusion.139
  95.9 2.6 %fusion.11 = bf16[64,512]{1,0:T(8,128)(2,1)S(1)} fusion(f32[64,512]{1,0:T(8,128)} %copy-done.8, bf16[2048,512]{1,0:T(8,128)(2,1)S(1)} %copy-done, bf16[512,2048]{1,0:T(8,128)(2,1)} %param.31, f32[512]{0:T(512)} %param.30, f32[64]{0:T(128)S(1)} %add_rsqrt_fusion.13, f32[64]{0:T(128)S(1)} %broadcast_multiply_fusion.6), kind=kOutput, calls=%fused_computation.27 | convolution fusion | flops 269811712 | bytes 4393472 | tf_op jit(solution)/shard_map/dot_general | solution.py:152
  99.5 3.5 %all-to-all-start.1 = ((bf16[16,2,1024]{2,1,0:T(2,128)(2,1)}), bf16[16,2,1024]{2,1,0:T(2,128)(2,1)S(1)}, u32[]{:S(2)}, u32[]{:S(2)}) async-start(bf16[16,2,1024]{2,1,0:T(2,128)(2,1)} %bitcast.22), calls=%async_computation.1 | async-start | bytes 131072 | tf_op jit(solution)/shard_map/all_to_all | solution.py:223
  104.3 5.5 %all-to-all-done.1 = bf16[16,2,1024]{2,1,0:T(2,128)(2,1)S(1)} async-done(((bf16[16,2,1024]{2,1,0:T(2,128)(2,1)}), bf16[16,2,1024]{2,1,0:T(2,128)(2,1)S(1)}, u32[]{:S(2)}, u32[]{:S(2)}) %all-to-all-start.1) | async-done | bytes 65568 | tf_op jit(solution)/shard_map/all_to_all | solution.py:223
  113.1 1.7 %mul.516 = f32[96,512]{1,0:T(8,128)} reshape(f32[32,3,512]{2,1,0:T(4,128)} %mul.515.clone) | data formatting | bytes 393216 | tf_op jit(solution)/shard_map/mul | solution.py:98
  115.5 1.7 %mul.525 = f32[96,512]{1,0:T(8,128)} reshape(f32[32,3,512]{2,1,0:T(4,128)} %mul.524.clone) | data formatting | bytes 393216 | tf_op jit(solution)/shard_map/mul | solution.py:99
  117.3 2.2 %fusion.6 = f32[96,500]{1,0:T(8,128)} fusion(bf16[512,500]{0,1:T(8,128)(2,1)} %param.35, f32[96,512]{1,0:T(8,128)S(1)} %add.248, f32[96,512]{1,0:T(8,128)} %mul.525, f32[96,512]{1,0:T(8,128)} %mul.516, f32[512]{0:T(512)} %param.34, f32[96]{0:T(128)S(1)} %rsqrt.134, f32[96]{0:T(128)S(1)} %div.166, f32[96]{0:T(128)} %mul.520, f32[96]{0:T(128)} %mul.462), kind=kOutput, calls=%fused_computation.16 | convolution fusion | flops 49641216 | bytes 1297408 | tf_op jit(solution)/shard_map/dot_general | solution.py:102
  119.5 1.0 reshape.619
  120.5 0.9 add_convert_fusion.1
  121.6 1.3 fusion.140
  124.1 1.2 fusion.143
  127.8 0.9 divide_convert_fusion.4
  130.9 1.0 reduce.9
  131.9 9.7 %all_to_all.16 = bf16[16,2,1024]{2,1,0:T(2,128)(2,1)S(1)} all-to-all(bf16[16,2,1024]{2,1,0:T(2,128)(2,1)S(1)} %reshape.634), channel_id=1, replica_groups=mesh['groups'=2,'lon'=16] {'lon'}, dimensions={0} | all-to-all | bytes 131072 | tf_op jit(solution)/shard_map/all_to_all | solution.py:206
  142.6 1.8 %fusion.74 = f32[64,1536]{1,0:T(8,128)S(1)} fusion(bf16[512,1536]{1,0:T(8,128)(2,1)} %param.28, f32[64,512]{1,0:T(8,128)S(1)} %reshape.621, f32[64]{0:T(128)S(1)} %add_rsqrt_fusion.12, f32[64]{0:T(128)S(1)} %broadcast_multiply_fusion.5, f32[512]{0:T(512)S(1)} %copy-done.20), kind=kOutput, calls=%fused_computation.142 | convolution fusion | flops 100794368 | bytes 2099712 | tf_op jit(solution)/shard_map/dot_general | solution.py:115
  147.2 1.0 reshape.606
  148.5 1.0 reshape.610
  150.5 1.2 convolution_convert_fusion
  152.5 2.5 %fusion.15 = bf16[64,512]{1,0:T(8,128)(2,1)S(1)} fusion(f32[64,512]{1,0:T(8,128)S(1)} %get-tuple-element.43, bf16[2048,512]{1,0:T(8,128)(2,1)S(1)} %copy-done, bf16[512,2048]{1,0:T(8,128)(2,1)} %param.31, f32[64]{0:T(128)S(1)} %add_rsqrt_fusion.11, f32[64]{0:T(128)S(1)} %broadcast_multiply_fusion.4, f32[512]{0:T(512)S(1)} %copy-done.21), kind=kOutput, calls=%fused_computation.31 | convolution fusion | flops 269811712 | bytes 4393472 | tf_op jit(solution)/shard_map/dot_general | solution.py:152
  155.4 9.5 %all_to_all.17 = bf16[16,2,1024]{2,1,0:T(2,128)(2,1)S(1)} all-to-all(bf16[16,2,1024]{2,1,0:T(2,128)(2,1)S(1)} %bitcast.151), channel_id=1, replica_groups=mesh['groups'=2,'lon'=16] {'lon'}, dimensions={0} | all-to-all | bytes 131072 | tf_op jit(solution)/shard_map/all_to_all | solution.py:223
  167.1 1.2 fusion.7
  (241 shorter events, 45.1 us)
Async XLA Ops:
  0.0 95.8 %copy-start = (bf16[2048,512]{1,0:T(8,128)(2,1)S(1)}, bf16[2048,512]{1,0:T(8,128)(2,1)}, u32[]{:S(2)}) copy-start(bf16[2048,512]{1,0:T(8,128)(2,1)} %param.32) | copy-start | bytes 6291460
  0.0 5.7 %copy-start.1 = (bf16[512,1024]{1,0:T(8,128)(2,1)S(1)}, bf16[512,1024]{1,0:T(8,128)(2,1)}, u32[]{:S(2)}) copy-start(bf16[512,1024]{1,0:T(8,128)(2,1)} %param.25) | copy-start | bytes 3145732
  20.9 0.6 copy-start.18
  28.2 18.0 %copy-start.26 = (f32[3,2]{0,1:T(2,128)S(1)}, f32[3,2]{0,1:T(2,128)}, u32[]{:S(2)}) copy-start(f32[3,2]{0,1:T(2,128)} %param.33) | copy-start | bytes 76
  28.2 18.0 %copy-start.27 = (s32[3]{0:T(128)S(1)}, s32[3]{0:T(128)}, u32[]{:S(2)}) copy-start(s32[3]{0:T(128)} %param.20) | copy-start | bytes 40
  28.9 15.5 %copy-start.13 = (f32[2,512]{1,0:T(2,128)}, f32[2,512]{1,0:T(2,128)S(1)}, u32[]{:S(2)}) copy-start(f32[2,512]{1,0:T(2,128)S(1)} %convert_element_type.247) | copy-start | bytes 12292
  36.7 14.4 %all-to-all-start = ((bf16[16,2,1024]{2,1,0:T(2,128)(2,1)}), bf16[16,2,1024]{2,1,0:T(2,128)(2,1)}, u32[]{:S(2)}, u32[]{:S(2)}) async-start(bf16[16,2,1024]{2,1,0:T(2,128)(2,1)} %reshape.632), calls=%async_computation | async-start | bytes 131072 | tf_op jit(solution)/shard_map/all_to_all | solution.py:206
  44.4 42.6 %copy-start.11 = (f32[64,64]{0,1:T(8,128)}, f32[64,64]{0,1:T(8,128)S(1)}, u32[]{:S(2)}) copy-start(f32[64,64]{0,1:T(8,128)S(1)} %compare_convert_fusion) | copy-start | bytes 49156
  46.3 71.0 %copy-start.6 = (f32[96,512]{1,0:T(8,128)}, f32[96,512]{1,0:T(8,128)S(1)}, u32[]{:S(2)}) copy-start(f32[96,512]{1,0:T(8,128)S(1)} %add.248) | copy-start | bytes 589828
  57.9 0.8 copy-start.2
  95.0 0.6 copy-start.8
  95.8 7.1 %copy-start.25 = (f32[3,2]{0,1:T(2,128)S(1)}, f32[3,2]{0,1:T(2,128)}, u32[]{:S(2)}) copy-start(f32[3,2]{0,1:T(2,128)} %fusion.118) | copy-start | bytes 76
  99.5 10.4 %all-to-all-start.1 = ((bf16[16,2,1024]{2,1,0:T(2,128)(2,1)}), bf16[16,2,1024]{2,1,0:T(2,128)(2,1)S(1)}, u32[]{:S(2)}, u32[]{:S(2)}) async-start(bf16[16,2,1024]{2,1,0:T(2,128)(2,1)} %bitcast.22), calls=%async_computation.1 | async-start | bytes 131072 | tf_op jit(solution)/shard_map/all_to_all | solution.py:223
  103.0 6.8 %copy-start.14 = (f32[3]{0:T(128)}, f32[3]{0:T(128)S(1)}, u32[]{:S(2)}) copy-start(f32[3]{0:T(128)S(1)} %get-tuple-element.34) | copy-start | bytes 40
  103.0 6.8 %copy-start.16 = (f32[3]{0:T(128)}, f32[3]{0:T(128)S(1)}, u32[]{:S(2)}) copy-start(f32[3]{0:T(128)S(1)} %get-tuple-element.35) | copy-start | bytes 40
  114.8 8.4 %copy-start.19 = (f32[512]{0:T(512)S(1)}, f32[512]{0:T(512)}, u32[]{:S(2)}) copy-start(f32[512]{0:T(512)} %param.23) | copy-start | bytes 6148
  121.4 1.9 %copy-start.9 = (bf16[1,32,1500]{2,1,0:T(8,128)(2,1)}, bf16[1,32,1500]{2,1,0:T(8,128)(2,1)S(1)}, u32[]{:S(2)}) copy-start(bf16[1,32,1500]{2,1,0:T(8,128)(2,1)S(1)} %add_convert_fusion.1) | copy-start | bytes 288004
  125.3 4.3 %copy-start.3 = (bf16[512,512]{1,0:T(8,128)(2,1)S(1)}, bf16[512,512]{1,0:T(8,128)(2,1)}, u32[]{:S(2)}) copy-start(bf16[512,512]{1,0:T(8,128)(2,1)} %param.26) | copy-start | bytes 1572868
  127.8 14.9 %copy-start.20 = (f32[512]{0:T(512)S(1)}, f32[512]{0:T(512)}, u32[]{:S(2)}) copy-start(f32[512]{0:T(512)} %param.27) | copy-start | bytes 6148
  145.6 4.7 %copy-start.12 = (f32[64,64]{0,1:T(8,128)S(1)}, f32[64,64]{0,1:T(8,128)}, u32[]{:S(2)}) copy-start(f32[64,64]{0,1:T(8,128)} %copy-done.11) | copy-start | bytes 49156
  146.5 5.4 %copy-start.4 = (bf16[512,512]{1,0:T(8,128)(2,1)S(1)}, bf16[512,512]{1,0:T(8,128)(2,1)}, u32[]{:S(2)}) copy-start(bf16[512,512]{1,0:T(8,128)(2,1)} %param.29) | copy-start | bytes 1572868
  148.1 4.3 %copy-start.21 = (f32[512]{0:T(512)S(1)}, f32[512]{0:T(512)}, u32[]{:S(2)}) copy-start(f32[512]{0:T(512)} %param.30) | copy-start | bytes 6148
  152.5 12.8 %copy-start.15 = (f32[3]{0:T(128)S(1)}, f32[3]{0:T(128)}, u32[]{:S(2)}) copy-start(f32[3]{0:T(128)} %copy-done.14) | copy-start | bytes 40
  152.5 12.8 %copy-start.17 = (f32[3]{0:T(128)S(1)}, f32[3]{0:T(128)}, u32[]{:S(2)}) copy-start(f32[3]{0:T(128)} %copy-done.16) | copy-start | bytes 40
  155.0 12.1 %copy-start.5 = (bf16[512,500]{0,1:T(8,128)(2,1)S(1)}, bf16[512,500]{0,1:T(8,128)(2,1)}, u32[]{:S(2)}) copy-start(bf16[512,500]{0,1:T(8,128)(2,1)} %param.35) | copy-start | bytes 1536004
  155.0 12.1 %copy-start.7 = (f32[96,512]{1,0:T(8,128)S(1)}, f32[96,512]{1,0:T(8,128)}, u32[]{:S(2)}) copy-start(f32[96,512]{1,0:T(8,128)} %copy-done.6) | copy-start | bytes 589828
  155.0 12.1 %copy-start.22 = (f32[512]{0:T(512)S(1)}, f32[512]{0:T(512)}, u32[]{:S(2)}) copy-start(f32[512]{0:T(512)} %param.34) | copy-start | bytes 6148
  155.0 12.1 %copy-start.23 = (f32[96]{0:T(128)S(1)}, f32[96]{0:T(128)}, u32[]{:S(2)}) copy-start(f32[96]{0:T(128)} %mul.462) | copy-start | bytes 1156
  155.1 12.0 %copy-start.24 = (f32[96]{0:T(128)S(1)}, f32[96]{0:T(128)}, u32[]{:S(2)}) copy-start(f32[96]{0:T(128)} %mul.520) | copy-start | bytes 1156
  165.1 3.3 %copy-start.10 = (bf16[1,32,1500]{2,1,0:T(8,128)(2,1)S(1)}, bf16[1,32,1500]{2,1,0:T(8,128)(2,1)}, u32[]{:S(2)}) copy-start(bf16[1,32,1500]{2,1,0:T(8,128)(2,1)} %copy-done.9) | copy-start | bytes 288004
where the time goes:
time: 172 us; the launch traced here: 169 us
  local copies, waits for them, and re-layouts  66.6 us (39%)
  matrix products  32.2 us (19%)
  other arithmetic  29.3 us (17%)
  blocking collectives  19.1 us (11%)
  starting transfers between devices  10.9 us (6%)
  waiting for transfers between devices  9.6 us (6%)
    mul x14, local copies, waits for them, and re-layouts, unit_heads(): return (shaped * lax.rsqrt(mean_square + head_eps)).reshape(values.shape)  10.2 us
    all_to_all x1, blocking collectives, shards(): lax.all_to_all(blocks.reshape(1, local_count, latent_width), 'lon', split...  9.66 us
    all_to_all x1, blocking collectives, shards(): lax.all_to_all(outgoing, 'lon', split_axis=0, concat_axis=1, tiled=True)  9.48 us
    all_to_all x1, starting transfers between devices, shards(): lax.all_to_all(blocks.reshape(1, local_count, latent_width), 'lon', split...  7.44 us
    reshape x6, local copies, waits for them, and re-layouts, to_windows(): head_data.reshape(lat_win, W_LAT, lon_win, W_LON, LATL, HEADS, head_dim)  6.95 us
    mul x7, local copies, waits for them, and re-layouts, unit_heads(): mean_square = jnp.mean(shaped * shaped, axis=-1, keepdims=True)  6.84 us
    transpose x6, local copies, waits for them, and re-layouts, to_windows(): shaped.transpose(0, 2, 5, 1, 3, 4, 6)  5.92 us
    all_to_all x1, waiting for transfers between devices, shards(): lax.all_to_all(outgoing, 'lon', split_axis=0, concat_axis=1, tiled=True)  5.53 us
  transfers between devices with their start and end apart: 2, of which 2 were waited for; matrix products, arithmetic and copies ran while one was open for 2% of the time, Pallas kernels for 0%

commit v1 on v0

v1 whole, which is shorter than its diff:
```python
import functools

import jax
import jax.numpy as jnp
from jax import lax
from jax.experimental import pallas as pl
from jax.experimental.pallas import tpu as pltpu
from jax.sharding import PartitionSpec as P

D = 512
HEADS = 8
HEAD = D // HEADS
HALF = D // 2
PIN = 500
PAD = 512
LEV = 3
LATL = 2
W_LAT = 4
W_LON = 8
STEPS = 2
ROW_PARTS = 4
WIN = W_LAT * W_LON
MESH = pl.DeviceIdType.MESH
F32 = jnp.float32
BF16 = jnp.bfloat16

norm_eps = 1e-05
head_eps = 1e-06


def mm(left, right):
    return jnp.dot(left, right, preferred_element_type=F32)


def layer_norm(values, scale_row):
    centred = values - jnp.mean(values, axis=-1, keepdims=True)
    spread = jnp.mean(centred * centred, axis=-1, keepdims=True)
    return centred * lax.rsqrt(spread + norm_eps) * scale_row


def head_sums(values, block):
    values = values.astype(BF16)
    return jnp.concatenate([mm(values[:, :HALF], block), mm(values[:, HALF:], block)], axis=1)


def kernel(
    n,
    lat_count,
    piece_cols,
    ids_ref,
    mix_ref,
    fields_ref,
    embed_ref,
    query_ref,
    enc_gain_ref,
    attn_gain_ref,
    mlp_gain_ref,
    dec_gain_ref,
    w_embed_hbm,
    w_kv_hbm,
    w_pool_hbm,
    w_qkv_hbm,
    w_proj_hbm,
    w_up_hbm,
    w_down_hbm,
    w_dec_hbm,
    out_ref,
    w_embed,
    w_kv,
    w_pool,
    w_qkv,
    w_proj,
    w_up,
    w_down,
    w_dec,
    rows32,
    work,
    send,
    recv,
    send_back,
    recv_back,
    weight_sem,
    send_sem,
    recv_sem,
    send_back_sem,
    recv_back_sem,
):
    me = lax.axis_index("lon")
    unroll = n <= 16
    lag = (W_LON // 2) // piece_cols
    half_rows = W_LAT // 2
    slots_win = WIN // piece_cols
    wide = LEV * PIN

    barrier = pltpu.get_barrier_semaphore()

    def greet(step, _):
        pl.semaphore_signal(
            barrier, inc=1, device_id={"lon": lax.rem(me + step, n)}, device_id_type=MESH
        )
        return 0

    lax.fori_loop(1, n, greet, 0, unroll=unroll)

    weights = [
        pltpu.make_async_copy(src, dst, weight_sem.at[i])
        for i, (src, dst) in enumerate(
            [
                (w_embed_hbm, w_embed),
                (w_kv_hbm, w_kv),
                (w_pool_hbm, w_pool),
                (w_qkv_hbm, w_qkv),
                (w_proj_hbm, w_proj),
                (w_up_hbm, w_up),
                (w_down_hbm, w_down),
                (w_dec_hbm, w_dec),
            ]
        )
    ]
    for copy in weights:
        copy.start()

    rows32[:, :wide] = fields_ref[0].astype(F32)

    group = 8 // piece_cols

    def pack(i, _):
        rows = rows32[pl.ds(pl.multiple_of(i * 8, 8), 8), :wide]
        for k in range(group):
            send[i * group + k] = rows[k * piece_cols : (k + 1) * piece_cols].astype(BF16)
        return 0

    lax.fori_loop(0, n // group, pack, 0, unroll=unroll)

    def place(device):
        piece = device // lat_count
        row = lax.rem(device, lat_count)
        shifted_row = lax.rem(row - half_rows + lat_count, lat_count)
        slot = shifted_row * ROW_PARTS + piece
        carry = (piece - lag + ROW_PARTS) // ROW_PARTS - 1
        return slot, carry

    my_slot, my_carry = place(me)

    pl.semaphore_wait(barrier, n - 1)

    def outward(step):
        target = lax.rem(me + step, n)
        return pltpu.make_async_remote_copy(
            src_ref=send.at[lax.rem(target - my_carry + n, n)],
            dst_ref=recv.at[my_slot],
            send_sem=send_sem,
            recv_sem=recv_sem,
            device_id={"lon": target},
            device_id_type=MESH,
        )

    def start_outward(step, _):
        outward(step).start()
        return 0

    lax.fori_loop(1, n, start_outward, 0, unroll=unroll)
    recv[my_slot] = send[lax.rem(me - my_carry + n, n)]

    embeds, mixes = [], []
    for l in range(LEV):
        row = jnp.zeros((1, D), F32)
        for k in range(LEV):
            hit = (ids_ref[l] == k).astype(F32)
            row = row + hit * embed_ref[k : k + 1, :].astype(F32)
        embeds.append(row)
        weights_l = []
        for j in range(LATL):
            total = jnp.float32(0.0)
            for k in range(LEV):
                total = total + (ids_ref[l] == k).astype(F32) * mix_ref[k, j]
            weights_l.append(total)
        mixes.append(weights_l)
    block = (
        lax.broadcasted_iota(jnp.int32, (HALF, HALF), 0) // HEAD
        == lax.broadcasted_iota(jnp.int32, (HALF, HALF), 1) // HEAD
    ).astype(BF16)
    query = query_ref[...].astype(F32)
    query_square = jnp.concatenate([query * query, jnp.zeros((6, D), F32)], axis=0)
    q_scale = lax.rsqrt(head_sums(query_square, block)[:LATL] * (1.0 / HEAD) + head_eps)
    q_unit = (query * q_scale).astype(BF16).astype(F32) * (HEAD**-0.5)

    def all_of(buffer, sem):
        part = buffer.at[pl.ds(0, n - 1)]
        return pltpu.make_async_copy(part, part, sem)

    all_of(recv, recv_sem).wait()

    lane = lax.broadcasted_iota(jnp.int32, (WIN, LEV * PAD), 1)

    def window(w, first):
        for i in range(slots_win):
            work[i * piece_cols : (i + 1) * piece_cols, :wide] = recv[w * slots_win + i].astype(F32)
        if first:
            weights[0].wait()
        flat = work[...]
        levels = [flat[:, :PIN]]
        for l in range(1, LEV):
            moved = pltpu.roll(flat, (PAD - PIN) * l, axis=1)
            levels.append(moved[:, l * PAD : l * PAD + PIN])
        current = jnp.concatenate(levels, axis=0).astype(BF16)

        shape = (LATL * WIN, HALF)
        token = lax.rem(lax.broadcasted_iota(jnp.int32, shape, 0), WIN)
        other = lax.rem(lax.broadcasted_iota(jnp.int32, shape, 1), WIN)
        edge = lat_count - half_rows
        region = (w * W_LAT + token // W_LON >= edge).astype(jnp.int32)
        region_other = (w * W_LAT + other // W_LON >= edge).astype(jnp.int32)
        allowed = (region == region_other).astype(F32)

        for step in range(STEPS):
            head = first and step == 0
            tokens = mm(current, w_embed[...])
            tokens = jnp.concatenate(
                [tokens[l * WIN : (l + 1) * WIN] + embeds[l] for l in range(LEV)], axis=0
            )
            tokens = layer_norm(tokens, enc_gain_ref[...]).astype(BF16)
            if head:
                weights[1].wait()
            keyval = mm(tokens, w_kv[...])
            keys, vals = keyval[:, :D], keyval[:, D:]
            k_scale = lax.rsqrt(head_sums(keys * keys, block) * (1.0 / HEAD) + head_eps)
            k_unit = keys * k_scale
            pooled = []
            for j in range(LATL):
                e = jnp.exp(head_sums(k_unit * q_unit[j : j + 1], block))
                top, bottom = 0.0, 0.0
                for l in range(LEV):
                    part = e[l * WIN : (l + 1) * WIN]
                    top = top + part * vals[l * WIN : (l + 1) * WIN]
                    bottom = bottom + part
                pooled.append(top / bottom)
            pooled = jnp.concatenate(pooled, axis=0).astype(BF16)
            if head:
                weights[2].wait()
            latents = mm(pooled, w_pool[...])
            latents = jnp.concatenate(
                [latents[j * WIN : (j + 1) * WIN] + query[j : j + 1] for j in range(LATL)], axis=0
            )
            latents = latents.astype(BF16).astype(F32)

            normed = layer_norm(latents, attn_gain_ref[...]).astype(BF16)
            if head:
                weights[3].wait()
            projected = mm(normed, w_qkv[...])
            wq, wk = projected[:, :D], projected[:, D : 2 * D]
            wv = projected[:, 2 * D :].astype(BF16)
            wq = wq * lax.rsqrt(head_sums(wq * wq, block) * (1.0 / HEAD) + head_eps)
            wk = wk * lax.rsqrt(head_sums(wk * wk, block) * (1.0 / HEAD) + head_eps)
            wq = (wq * (HEAD**-0.5)).astype(BF16)
            wk = wk.astype(BF16)
            mixed = []
            for s in range(2):
                side = slice(s * HALF, (s + 1) * HALF)
                big_k = jnp.concatenate([wk[:, side]] * (HALF // HEAD), axis=0) * block
                big_v = jnp.concatenate([wv[:, side]] * (HALF // HEAD), axis=0) * block
                scores = lax.dot_general(
                    wq[:, side], big_k, (((1,), (1,)), ((), ())), preferred_element_type=F32
                )
                e = (jnp.exp(scores) * allowed).astype(BF16)
                mixed.append(mm(e, big_v) / mm(e, block))
            mixed = jnp.concatenate(mixed, axis=1).astype(BF16)
            if head:
                weights[4].wait()
            attended = (latents + mm(mixed, w_proj[...])).astype(BF16).astype(F32)

            normed = layer_norm(attended, mlp_gain_ref[...]).astype(BF16)
            if head:
                weights[5].wait()
            hidden = jax.nn.gelu(mm(normed, w_up[...])).astype(BF16)
            if head:
                weights[6].wait()
            backbone = (attended + mm(hidden, w_down[...])).astype(BF16).astype(F32)

            blended = jnp.concatenate(
                [
                    mixes[l][0] * backbone[:WIN] + mixes[l][1] * backbone[WIN:] + embeds[l]
                    for l in range(LEV)
                ],
                axis=0,
            )
            decoded = layer_norm(blended, dec_gain_ref[...]).astype(BF16)
            if head:
                weights[7].wait()
            added = mm(decoded, w_dec[...]).astype(BF16)
            current = (current.astype(F32) + added.astype(F32)).astype(BF16)

        final = current.astype(F32)
        for l in range(LEV):
            work[:, l * PAD : l * PAD + PIN] = final[l * WIN : (l + 1) * WIN]
        flat = work[...]
        merged = flat
        for l in range(1, LEV):
            moved = pltpu.roll(flat, LEV * PAD - (PAD - PIN) * l, axis=1)
            merged = jnp.where(lane >= l * PIN, moved, merged)
        work[...] = merged
        for i in range(slots_win):
            send_back[w * slots_win + i] = work[
                i * piece_cols : (i + 1) * piece_cols, :wide
            ].astype(BF16)

    window(0, True)
    windows = lat_count // W_LAT
    if windows > 1:

        def more(w, _):
            window(w, False)
            return 0

        lax.fori_loop(1, windows, more, 0)

    def start_back(step, _):
        target = lax.rem(me + step, n)
        slot, carry = place(target)
        pltpu.make_async_remote_copy(
            src_ref=send_back.at[slot],
            dst_ref=recv_back.at[lax.rem(me - carry + n, n)],
            send_sem=send_back_sem,
            recv_sem=recv_back_sem,
            device_id={"lon": target},
            device_id_type=MESH,
        ).start()
        return 0

    lax.fori_loop(1, n, start_back, 0, unroll=unroll)
    recv_back[lax.rem(me - my_carry + n, n)] = send_back[my_slot]
    all_of(send, send_sem).wait()
    all_of(recv_back, recv_back_sem).wait()

    def unpack(i, _):
        rows = [recv_back[i * group + k].astype(F32) for k in range(group)]
        rows32[pl.ds(pl.multiple_of(i * 8, 8), 8), :wide] = jnp.concatenate(rows, axis=0)
        return 0

    lax.fori_loop(0, n // group, unpack, 0, unroll=unroll)
    out_ref[0] = rows32[:, :wide].astype(BF16)
    all_of(send_back, send_back_sem).wait()


def shards(
    n,
    fields,
    level_ids,
    embed_weight,
    level_embed,
    enc_gain,
    latent_query,
    kv_weight,
    pool_out,
    attn_gain,
    qkv_weight,
    attn_proj,
    mlp_gain,
    mlp_up,
    mlp_down,
    level_mix,
    dec_gain,
    dec_weight,
):
    local_count = fields.shape[1]
    wide = fields.shape[2]
    piece_cols = local_count // n
    lat_count = n // ROW_PARTS
    smem = pl.BlockSpec(memory_space=pltpu.SMEM)
    vmem = pl.BlockSpec(memory_space=pltpu.VMEM)
    any_space = pl.BlockSpec(memory_space=pl.ANY)
    matrices = (
        embed_weight,
        kv_weight,
        pool_out,
        qkv_weight,
        attn_proj,
        mlp_up,
        mlp_down,
        dec_weight,
    )
    return pl.pallas_call(
        functools.partial(kernel, n, lat_count, piece_cols),
        name="forecast",
        out_shape=jax.ShapeDtypeStruct(fields.shape, BF16),
        in_specs=[smem] * 2 + [vmem] * 7 + [any_space] * len(matrices),
        out_specs=vmem,
        scratch_shapes=[pltpu.VMEM(m.shape, BF16) for m in matrices]
        + [
            pltpu.VMEM((local_count, LEV * PAD), F32),
            pltpu.VMEM((WIN, LEV * PAD), F32),
            pltpu.VMEM((n, piece_cols, wide), BF16),
            pltpu.VMEM((n, piece_cols, wide), BF16),
            pltpu.VMEM((n, piece_cols, wide), BF16),
            pltpu.VMEM((n, piece_cols, wide), BF16),
            pltpu.SemaphoreType.DMA((len(matrices),)),
            pltpu.SemaphoreType.DMA,
            pltpu.SemaphoreType.DMA,
            pltpu.SemaphoreType.DMA,
            pltpu.SemaphoreType.DMA,
        ],
        compiler_params=pltpu.CompilerParams(
            collective_id=0, has_side_effects=True, vmem_limit_bytes=48 * 1024 * 1024
        ),
    )(
        level_ids,
        level_mix,
        fields,
        level_embed,
        latent_query,
        enc_gain.reshape(1, D),
        attn_gain.reshape(1, D),
        mlp_gain.reshape(1, D),
        dec_gain.reshape(1, D),
        *matrices,
    )


def solution(mesh):
    rep = P()
    rows = P(("groups", "lon"), None, None)
    return jax.shard_map(
        functools.partial(shards, mesh.shape["lon"]),
        mesh=mesh,
        in_specs=(rows, P("groups")) + (rep,) * 15,
        out_specs=rows,
        check_vma=False,
    )
```

time: 172 us -> 38.1 us (0.22); the launches traced: 169 us -> 37.5 us
  local copies, waits for them, and re-layouts: 66.6 us -> 14 us
  matrix products: 32.2 us -> 0 us
  other arithmetic: 29.3 us -> 0 us
  Pallas kernels: 0 us -> 23.4 us
  blocking collectives: 19.1 us -> 0 us
  starting transfers between devices: 10.9 us -> 0 us
  waiting for transfers between devices: 9.6 us -> 0 us
    dot_general x24 -> x0, matrix products: 32.2 us -> none  [the longest x4 5.2 us: product(): jnp.einsum(einsum_form, left_side, right_side, preferred_element_type=jnp...]
    mul x34 -> x0, local copies, waits for them, and re-layouts: 24.2 us -> none  [the longest x14 10.2 us: unit_heads(): return (shaped * lax.rsqrt(mean_square + head_eps)).reshape(values.shape)]
    pallas_call x0 -> x1, Pallas kernels: none -> 23.4 us  [shards(): pl.pallas_call(functools.partial(kernel, n, lat_count, piece_cols), name=...]
    all_to_all x2 -> x0, blocking collectives: 19.1 us -> none  [the longest x1 9.66 us: shards(): lax.all_to_all(blocks.reshape(1, local_count, latent_width), 'lon', split...]
    reshape x18 -> x0, local copies, waits for them, and re-layouts: 12.6 us -> none  [the longest x6 6.95 us: to_windows(): head_data.reshape(lat_win, W_LAT, lon_win, W_LON, LATL, HEADS, head_dim)]
    all_to_all x2 -> x0, starting transfers between devices: 10.9 us -> none  [the longest x1 7.44 us: shards(): lax.all_to_all(blocks.reshape(1, local_count, latent_width), 'lon', split...]
    unnamed x66 -> x29, local copies, waits for them, and re-layouts: 3.62 us -> 14 us
    all_to_all x2 -> x0, waiting for transfers between devices: 9.6 us -> none  [the longest x1 5.53 us: shards(): lax.all_to_all(outgoing, 'lon', split_axis=0, concat_axis=1, tiled=True)]
  transfers between devices with their start and end apart: 2 -> 0, of which waited for: 2 -> 0; matrix products, arithmetic and copies ran while one was open for 2% -> 0% of each run, Pallas kernels for 0% -> 0%
where the time goes in v1:
time: 38.1 us; the launch traced here: 37.5 us
  Pallas kernels  23.4 us (61%)
  local copies, waits for them, and re-layouts  14 us (37%)
    pallas_call x1, Pallas kernels, shards(): pl.pallas_call(functools.partial(kernel, n, lat_count, piece_cols), name=...  23.4 us
    unnamed x29, local copies, waits for them, and re-layouts  14 us

profile of v1, /device:TPU:0, one launch (start us, length us, event | category | flops | bytes accessed | tf_op | source)
XLA Modules:
  0.0 37.5 jit_solution(17852058842439693940)
XLA Ops:
  0.0 0.8 %copy.18.mix_ref = f32[3,2]{1,0:T(4,128)S(1)} copy(f32[3,2]{0,1:T(2,128)} %param.31) | data formatting | bytes 48 | tf_op args[14]
  0.8 1.2 %copy.19.w_dec_hbm = bf16[512,500]{1,0:T(8,128)(2,1)S(1)} copy(bf16[512,500]{0,1:T(8,128)(2,1)} %param.33) | data formatting | bytes 1024000 | tf_op args[16]
  2.0 0.0 copy-start
  2.0 1.4 %copy-done = bf16[512,1536]{1,0:T(8,128)(2,1)S(1)} copy-done((bf16[512,1536]{1,0:T(8,128)(2,1)S(1)}, bf16[512,1536]{1,0:T(8,128)(2,1)}, u32[]{:S(2)}) %copy-start) | copy-done | bytes 1572888
  3.4 0.0 copy-start.1
  3.4 1.2 %copy-done.1 = bf16[512,1024]{1,0:T(8,128)(2,1)S(1)} copy-done((bf16[512,1024]{1,0:T(8,128)(2,1)S(1)}, bf16[512,1024]{1,0:T(8,128)(2,1)}, u32[]{:S(2)}) %copy-start.1) | copy-done | bytes 1048600
  4.7 0.0 copy-start.2
  4.7 1.0 %copy-done.2 = bf16[512,512]{1,0:T(8,128)(2,1)S(1)} copy-done((bf16[512,512]{1,0:T(8,128)(2,1)S(1)}, bf16[512,512]{1,0:T(8,128)(2,1)}, u32[]{:S(2)}) %copy-start.2) | copy-done | bytes 524312
  5.7 0.0 copy-start.3
  5.7 1.0 %copy-done.3 = bf16[512,512]{1,0:T(8,128)(2,1)S(1)} copy-done((bf16[512,512]{1,0:T(8,128)(2,1)S(1)}, bf16[512,512]{1,0:T(8,128)(2,1)}, u32[]{:S(2)}) %copy-start.3) | copy-done | bytes 524312
  6.7 0.0 copy-start.4
  6.7 1.0 %copy-done.4 = bf16[500,512]{1,0:T(8,128)(2,1)S(1)} copy-done((bf16[500,512]{1,0:T(8,128)(2,1)S(1)}, bf16[500,512]{1,0:T(8,128)(2,1)}, u32[]{:S(2)}) %copy-start.4) | copy-done | bytes 512024
  7.8 0.0 copy-start.5
  7.8 0.9 %copy-done.5 = bf16[1,32,1500]{2,1,0:T(8,128)(2,1)S(1)} copy-done((bf16[1,32,1500]{2,1,0:T(8,128)(2,1)S(1)}, bf16[1,32,1500]{2,1,0:T(8,128)(2,1)}, u32[]{:S(2)}) %copy-start.5) | copy-done | bytes 96024
  8.7 0.0 copy-start.6
  8.7 0.7 %copy-done.6 = bf16[3,512]{1,0:T(4,128)(2,1)S(1)} copy-done((bf16[3,512]{1,0:T(4,128)(2,1)S(1)}, bf16[3,512]{1,0:T(4,128)(2,1)}, u32[]{:S(2)}) %copy-start.6) | copy-done | bytes 3096
  9.4 0.0 copy-start.7
  9.4 0.7 %copy-done.7 = bf16[2,512]{1,0:T(2,128)(2,1)S(1)} copy-done((bf16[2,512]{1,0:T(2,128)(2,1)S(1)}, bf16[2,512]{1,0:T(2,128)(2,1)}, u32[]{:S(2)}) %copy-start.7) | copy-done | bytes 2072
  10.0 0.0 copy-start.8
  10.0 0.7 %copy-done.8 = f32[512]{0:T(512)S(1)} copy-done((f32[512]{0:T(512)S(1)}, f32[512]{0:T(512)}, u32[]{:S(2)}) %copy-start.8) | copy-done | bytes 2072
  10.7 0.0 copy-start.9
  10.7 0.7 %copy-done.9 = f32[512]{0:T(512)S(1)} copy-done((f32[512]{0:T(512)S(1)}, f32[512]{0:T(512)}, u32[]{:S(2)}) %copy-start.9) | copy-done | bytes 2072
  11.4 0.0 copy-start.10
  11.4 0.7 %copy-done.10 = f32[512]{0:T(512)S(1)} copy-done((f32[512]{0:T(512)S(1)}, f32[512]{0:T(512)}, u32[]{:S(2)}) %copy-start.10) | copy-done | bytes 2072
  12.1 0.0 copy-start.11
  12.1 0.7 %copy-done.11 = f32[512]{0:T(512)S(1)} copy-done((f32[512]{0:T(512)S(1)}, f32[512]{0:T(512)}, u32[]{:S(2)}) %copy-start.11) | copy-done | bytes 2072
  12.8 0.0 copy-start.12
  12.8 0.7 %copy-done.12 = s32[3]{0:T(128)S(1)} copy-done((s32[3]{0:T(128)S(1)}, s32[3]{0:T(128)}, u32[]{:S(2)}) %copy-start.12) | copy-done | bytes 36
  13.4 23.4 %forecast.1 = bf16[1,32,1500]{2,1,0:T(8,128)(2,1)S(1)} custom-call(s32[3]{0:T(128)S(1)} %copy-done.12, f32[3,2]{1,0:T(4,128)S(1)} %copy.18.mix_ref, bf16[1,32,1500]{2,1,0:T(8,128)(2,1)S(1)} %copy-done.5, bf16[3,512]{1,0:T(4,128)(2,1)S(1)} %copy-done.6, bf16[2,512]{1,0:T(2,128)(2,1)S(1)} %copy-done.7, f32[1,512]{1,0:T(1,128)S(1)} %bitcast.4, ...), custom_call_target="tpu_custom_call" | custom-call | tf_op jit(solution)/shard_map/forecast/pallas_call | solution.py:382
  36.9 0.6 %copy.21 = bf16[1,32,1500]{2,1,0:T(8,128)(2,1)} copy(bf16[1,32,1500]{2,1,0:T(8,128)(2,1)S(1)} %forecast.1) | data formatting | bytes 192000
Async XLA Ops:
  2.0 1.4 %copy-start = (bf16[512,1536]{1,0:T(8,128)(2,1)S(1)}, bf16[512,1536]{1,0:T(8,128)(2,1)}, u32[]{:S(2)}) copy-start(bf16[512,1536]{1,0:T(8,128)(2,1)} %w_qkv_hbm.1) | copy-start | bytes 4718596
  3.4 1.2 %copy-start.1 = (bf16[512,1024]{1,0:T(8,128)(2,1)S(1)}, bf16[512,1024]{1,0:T(8,128)(2,1)}, u32[]{:S(2)}) copy-start(bf16[512,1024]{1,0:T(8,128)(2,1)} %w_kv_hbm.1) | copy-start | bytes 3145732
  4.7 1.0 %copy-start.2 = (bf16[512,512]{1,0:T(8,128)(2,1)S(1)}, bf16[512,512]{1,0:T(8,128)(2,1)}, u32[]{:S(2)}) copy-start(bf16[512,512]{1,0:T(8,128)(2,1)} %w_pool_hbm.1) | copy-start | bytes 1572868
  5.7 1.0 %copy-start.3 = (bf16[512,512]{1,0:T(8,128)(2,1)S(1)}, bf16[512,512]{1,0:T(8,128)(2,1)}, u32[]{:S(2)}) copy-start(bf16[512,512]{1,0:T(8,128)(2,1)} %w_proj_hbm.1) | copy-start | bytes 1572868
  6.7 1.0 %copy-start.4 = (bf16[500,512]{1,0:T(8,128)(2,1)S(1)}, bf16[500,512]{1,0:T(8,128)(2,1)}, u32[]{:S(2)}) copy-start(bf16[500,512]{1,0:T(8,128)(2,1)} %w_embed_hbm.1) | copy-start | bytes 1536004
  7.8 0.9 %copy-start.5 = (bf16[1,32,1500]{2,1,0:T(8,128)(2,1)S(1)}, bf16[1,32,1500]{2,1,0:T(8,128)(2,1)}, u32[]{:S(2)}) copy-start(bf16[1,32,1500]{2,1,0:T(8,128)(2,1)} %fields_ref.1) | copy-start | bytes 288004
  8.7 0.7 %copy-start.6 = (bf16[3,512]{1,0:T(4,128)(2,1)S(1)}, bf16[3,512]{1,0:T(4,128)(2,1)}, u32[]{:S(2)}) copy-start(bf16[3,512]{1,0:T(4,128)(2,1)} %embed_ref.1) | copy-start | bytes 9220
  9.4 0.7 %copy-start.7 = (bf16[2,512]{1,0:T(2,128)(2,1)S(1)}, bf16[2,512]{1,0:T(2,128)(2,1)}, u32[]{:S(2)}) copy-start(bf16[2,512]{1,0:T(2,128)(2,1)} %query_ref.1) | copy-start | bytes 6148
  10.0 0.7 %copy-start.8 = (f32[512]{0:T(512)S(1)}, f32[512]{0:T(512)}, u32[]{:S(2)}) copy-start(f32[512]{0:T(512)} %param.21) | copy-start | bytes 6148
  10.7 0.7 %copy-start.9 = (f32[512]{0:T(512)S(1)}, f32[512]{0:T(512)}, u32[]{:S(2)}) copy-start(f32[512]{0:T(512)} %param.25) | copy-start | bytes 6148
  11.4 0.7 %copy-start.10 = (f32[512]{0:T(512)S(1)}, f32[512]{0:T(512)}, u32[]{:S(2)}) copy-start(f32[512]{0:T(512)} %param.28) | copy-start | bytes 6148
  12.1 0.7 %copy-start.11 = (f32[512]{0:T(512)S(1)}, f32[512]{0:T(512)}, u32[]{:S(2)}) copy-start(f32[512]{0:T(512)} %param.32) | copy-start | bytes 6148
  12.8 0.7 %copy-start.12 = (s32[3]{0:T(128)S(1)}, s32[3]{0:T(128)}, u32[]{:S(2)}) copy-start(s32[3]{0:T(128)} %ids_ref.1) | copy-start | bytes 40

commit v2 on v1

--- a/solution.py
+++ b/solution.py
@@ -24,6 +24,8 @@
 F32 = jnp.float32
 BF16 = jnp.bfloat16
 
+OPERANDS = (pltpu.VMEM, pltpu.SMEM, pltpu.SMEM) + (pltpu.VMEM,) * 14
+
 norm_eps = 1e-05
 head_eps = 1e-06
 
@@ -47,44 +49,21 @@
     n,
     lat_count,
     piece_cols,
-    ids_ref,
-    mix_ref,
-    fields_ref,
-    embed_ref,
-    query_ref,
-    enc_gain_ref,
-    attn_gain_ref,
-    mlp_gain_ref,
-    dec_gain_ref,
-    w_embed_hbm,
-    w_kv_hbm,
-    w_pool_hbm,
-    w_qkv_hbm,
-    w_proj_hbm,
-    w_up_hbm,
-    w_down_hbm,
-    w_dec_hbm,
-    out_ref,
-    w_embed,
-    w_kv,
-    w_pool,
-    w_qkv,
-    w_proj,
-    w_up,
-    w_down,
-    w_dec,
-    rows32,
-    work,
-    send,
-    recv,
-    send_back,
-    recv_back,
-    weight_sem,
-    send_sem,
-    recv_sem,
-    send_back_sem,
-    recv_back_sem,
+    *refs,
 ):
+    count = len(OPERANDS)
+    sources, out_ref, landed, scratch = (
+        refs[:count],
+        refs[count],
+        refs[count + 1 : 2 * count + 1],
+        refs[2 * count + 1 :],
+    )
+    fields_ref, ids_ref, mix_ref, embed_ref, query_ref = landed[:5]
+    enc_gain_ref, attn_gain_ref, mlp_gain_ref, dec_gain_ref = landed[5:9]
+    w_embed, w_kv, w_pool, w_qkv, w_proj, w_up, w_down, w_dec = landed[9:]
+    rows32, work, send, recv, send_back, recv_back = scratch[:6]
+    load_sem, send_sem, recv_sem, send_back_sem, recv_back_sem = scratch[6:]
+
     me = lax.axis_index("lon")
     unroll = n <= 16
     lag = (W_LON // 2) // piece_cols
@@ -92,6 +71,14 @@
     slots_win = WIN // piece_cols
     wide = LEV * PIN
 
+    loads = [
+        pltpu.make_async_copy(src, dst, load_sem.at[i])
+        for i, (src, dst) in enumerate(zip(sources, landed))
+    ]
+    for copy in loads:
+        copy.start()
+    weights = loads[9:]
+
     barrier = pltpu.get_barrier_semaphore()
 
     def greet(step, _):
@@ -102,24 +89,7 @@
 
     lax.fori_loop(1, n, greet, 0, unroll=unroll)
 
-    weights = [
-        pltpu.make_async_copy(src, dst, weight_sem.at[i])
-        for i, (src, dst) in enumerate(
-            [
-                (w_embed_hbm, w_embed),
-                (w_kv_hbm, w_kv),
-                (w_pool_hbm, w_pool),
-                (w_qkv_hbm, w_qkv),
-                (w_proj_hbm, w_proj),
-                (w_up_hbm, w_up),
-                (w_down_hbm, w_down),
-                (w_dec_hbm, w_dec),
-            ]
-        )
-    ]
-    for copy in weights:
-        copy.start()
-
+    loads[0].wait()
     rows32[:, :wide] = fields_ref[0].astype(F32)
 
     group = 8 // piece_cols
@@ -162,6 +132,8 @@
     lax.fori_loop(1, n, start_outward, 0, unroll=unroll)
     recv[my_slot] = send[lax.rem(me - my_carry + n, n)]
 
+    for copy in loads[1:9]:
+        copy.wait()
     embeds, mixes = [], []
     for l in range(LEV):
         row = jnp.zeros((1, D), F32)
@@ -173,7 +145,7 @@
         for j in range(LATL):
             total = jnp.float32(0.0)
             for k in range(LEV):
-                total = total + (ids_ref[l] == k).astype(F32) * mix_ref[k, j]
+                total = total + (ids_ref[l] == k).astype(F32) * mix_ref[j, k]
             weights_l.append(total)
         mixes.append(weights_l)
     block = (
@@ -287,7 +259,9 @@
             decoded = layer_norm(blended, dec_gain_ref[...]).astype(BF16)
             if head:
                 weights[7].wait()
-            added = mm(decoded, w_dec[...]).astype(BF16)
+            added = lax.dot_general(
+                decoded, w_dec[...], (((1,), (1,)), ((), ())), preferred_element_type=F32
+            ).astype(BF16)
             current = (current.astype(F32) + added.astype(F32)).astype(BF16)
 
         final = current.astype(F32)
@@ -366,10 +340,16 @@
     wide = fields.shape[2]
     piece_cols = local_count // n
     lat_count = n // ROW_PARTS
-    smem = pl.BlockSpec(memory_space=pltpu.SMEM)
-    vmem = pl.BlockSpec(memory_space=pltpu.VMEM)
-    any_space = pl.BlockSpec(memory_space=pl.ANY)
-    matrices = (
+    operands = (
+        fields,
+        level_ids,
+        level_mix.T,
+        level_embed,
+        latent_query,
+        enc_gain.reshape(1, D),
+        attn_gain.reshape(1, D),
+        mlp_gain.reshape(1, D),
+        dec_gain.reshape(1, D),
         embed_weight,
         kv_weight,
         pool_out,
@@ -377,15 +357,18 @@
         attn_proj,
         mlp_up,
         mlp_down,
-        dec_weight,
+        dec_weight.T,
     )
+    operands = tuple(pltpu.with_memory_space_constraint(x, pltpu.HBM) for x in operands)
     return pl.pallas_call(
         functools.partial(kernel, n, lat_count, piece_cols),
         name="forecast",
         out_shape=jax.ShapeDtypeStruct(fields.shape, BF16),
-        in_specs=[smem] * 2 + [vmem] * 7 + [any_space] * len(matrices),
-        out_specs=vmem,
-        scratch_shapes=[pltpu.VMEM(m.shape, BF16) for m in matrices]
+        in_specs=[pl.BlockSpec(memory_space=pltpu.HBM)] * len(operands),
+        out_specs=pl.BlockSpec(memory_space=pltpu.VMEM),
+        scratch_shapes=[
+            space(x.shape, x.dtype) for space, x in zip(OPERANDS, operands, strict=True)
+        ]
         + [
             pltpu.VMEM((local_count, LEV * PAD), F32),
             pltpu.VMEM((WIN, LEV * PAD), F32),
@@ -393,7 +376,7 @@
             pltpu.VMEM((n, piece_cols, wide), BF16),
             pltpu.VMEM((n, piece_cols, wide), BF16),
             pltpu.VMEM((n, piece_cols, wide), BF16),
-            pltpu.SemaphoreType.DMA((len(matrices),)),
+            pltpu.SemaphoreType.DMA((len(operands),)),
             pltpu.SemaphoreType.DMA,
             pltpu.SemaphoreType.DMA,
             pltpu.SemaphoreType.DMA,
@@ -402,18 +385,7 @@
         compiler_params=pltpu.CompilerParams(
             collective_id=0, has_side_effects=True, vmem_limit_bytes=48 * 1024 * 1024
         ),
-    )(
-        level_ids,
-        level_mix,
-        fields,
-        level_embed,
-        latent_query,
-        enc_gain.reshape(1, D),
-        attn_gain.reshape(1, D),
-        mlp_gain.reshape(1, D),
-        dec_gain.reshape(1, D),
-        *matrices,
-    )
+    )(*operands)
 
 
 def solution(mesh):

time: 38.1 us -> 23.9 us (0.63); the launches traced: 37.5 us -> 23.7 us
  local copies, waits for them, and re-layouts: 14 us -> 0.64 us
    unnamed x29 -> x1, local copies, waits for them, and re-layouts: 14 us -> 0.64 us
where the time goes in v2:
time: 23.9 us; the launch traced here: 23.7 us
  Pallas kernels  23.1 us (97%)
  local copies, waits for them, and re-layouts  0.64 us (3%)
    pallas_call x1, Pallas kernels, shards(): pl.pallas_call(functools.partial(kernel, n, lat_count, piece_cols), name=...  23.1 us
    unnamed x1, local copies, waits for them, and re-layouts  0.64 us

profile of v2, /device:TPU:0, one launch (start us, length us, event | category | flops | bytes accessed | tf_op | source)
XLA Modules:
  0.0 23.7 jit_solution(7339298059931428437)
XLA Ops:
  0.0 23.1 %forecast.1 = bf16[1,32,1500]{2,1,0:T(8,128)(2,1)S(1)} custom-call(bf16[1,32,1500]{2,1,0:T(8,128)(2,1)} %refs_0_.1, s32[3]{0:T(128)} %refs_1_.1, f32[2,3]{1,0:T(2,128)} %bitcast.11, bf16[3,512]{1,0:T(4,128)(2,1)} %refs_3_.1, bf16[2,512]{1,0:T(2,128)(2,1)} %refs_4_.1, f32[1,512]{1,0:T(1,128)} %bitcast.7, f32[1,512]{1,0:T(1,128)} %bitcast.8, ...), custom_call_target="tpu_custom_call" | custom-call | tf_op jit(solution)/shard_map/forecast/pallas_call | solution.py:363
  23.1 0.6 %copy.19 = bf16[1,32,1500]{2,1,0:T(8,128)(2,1)} copy(bf16[1,32,1500]{2,1,0:T(8,128)(2,1)S(1)} %forecast.1) | data formatting | bytes 192000

commit v3 on v2

--- a/solution.py
+++ b/solution.py
@@ -62,7 +62,8 @@
     enc_gain_ref, attn_gain_ref, mlp_gain_ref, dec_gain_ref = landed[5:9]
     w_embed, w_kv, w_pool, w_qkv, w_proj, w_up, w_down, w_dec = landed[9:]
     rows32, work, send, recv, send_back, recv_back = scratch[:6]
-    load_sem, send_sem, recv_sem, send_back_sem, recv_back_sem = scratch[6:]
+    w_dec_t, send_lat, recv_lat, lat_send_sem, lat_recv_sem = scratch[6:11]
+    load_sem, send_sem, recv_sem, send_back_sem, recv_back_sem = scratch[11:]
 
     me = lax.axis_index("lon")
     unroll = n <= 16
@@ -70,6 +71,16 @@
     half_rows = W_LAT // 2
     slots_win = WIN // piece_cols
     wide = LEV * PIN
+
+    barrier = pltpu.get_barrier_semaphore()
+
+    def greet(step, _):
+        pl.semaphore_signal(
+            barrier, inc=1, device_id={"lon": lax.rem(me + step, n)}, device_id_type=MESH
+        )
+        return 0
+
+    lax.fori_loop(1, n, greet, 0, unroll=unroll)
 
     loads = [
         pltpu.make_async_copy(src, dst, load_sem.at[i])
@@ -79,23 +90,14 @@
         copy.start()
     weights = loads[9:]
 
-    barrier = pltpu.get_barrier_semaphore()
-
-    def greet(step, _):
-        pl.semaphore_signal(
-            barrier, inc=1, device_id={"lon": lax.rem(me + step, n)}, device_id_type=MESH
-        )
-        return 0
-
-    lax.fori_loop(1, n, greet, 0, unroll=unroll)
-
     loads[0].wait()
+    rows32[:, wide:] = jnp.zeros_like(rows32[:, wide:])
     rows32[:, :wide] = fields_ref[0].astype(F32)
 
     group = 8 // piece_cols
 
     def pack(i, _):
-        rows = rows32[pl.ds(pl.multiple_of(i * 8, 8), 8), :wide]
+        rows = rows32[pl.ds(pl.multiple_of(i * 8, 8), 8), :]
         for k in range(group):
             send[i * group + k] = rows[k * piece_cols : (k + 1) * piece_cols].astype(BF16)
         return 0
@@ -111,26 +113,6 @@
         return slot, carry
 
     my_slot, my_carry = place(me)
-
-    pl.semaphore_wait(barrier, n - 1)
-
-    def outward(step):
-        target = lax.rem(me + step, n)
-        return pltpu.make_async_remote_copy(
-            src_ref=send.at[lax.rem(target - my_carry + n, n)],
-            dst_ref=recv.at[my_slot],
-            send_sem=send_sem,
-            recv_sem=recv_sem,
-            device_id={"lon": target},
-            device_id_type=MESH,
-        )
-
-    def start_outward(step, _):
-        outward(step).start()
-        return 0
-
-    lax.fori_loop(1, n, start_outward, 0, unroll=unroll)
-    recv[my_slot] = send[lax.rem(me - my_carry + n, n)]
 
     for copy in loads[1:9]:
         copy.wait()
@@ -157,26 +139,101 @@
     q_scale = lax.rsqrt(head_sums(query_square, block)[:LATL] * (1.0 / HEAD) + head_eps)
     q_unit = (query * q_scale).astype(BF16).astype(F32) * (HEAD**-0.5)
 
-    def all_of(buffer, sem):
-        part = buffer.at[pl.ds(0, n - 1)]
-        return pltpu.make_async_copy(part, part, sem)
-
-    all_of(recv, recv_sem).wait()
-
-    lane = lax.broadcasted_iota(jnp.int32, (WIN, LEV * PAD), 1)
-
-    def window(w, first):
-        for i in range(slots_win):
-            work[i * piece_cols : (i + 1) * piece_cols, :wide] = recv[w * slots_win + i].astype(F32)
-        if first:
-            weights[0].wait()
-        flat = work[...]
+    def split_levels(flat):
         levels = [flat[:, :PIN]]
         for l in range(1, LEV):
             moved = pltpu.roll(flat, (PAD - PIN) * l, axis=1)
             levels.append(moved[:, l * PAD : l * PAD + PIN])
-        current = jnp.concatenate(levels, axis=0).astype(BF16)
-
+        return jnp.concatenate(levels, axis=0).astype(BF16)
+
+    def encode(current, head):
+        if head:
+            weights[0].wait()
+        tokens = mm(current, w_embed[...])
+        tokens = jnp.concatenate(
+            [tokens[l * WIN : (l + 1) * WIN] + embeds[l] for l in range(LEV)], axis=0
+        )
+        tokens = layer_norm(tokens, enc_gain_ref[...]).astype(BF16)
+        if head:
+            weights[1].wait()
+        keyval = mm(tokens, w_kv[...])
+        keys, vals = keyval[:, :D], keyval[:, D:]
+        k_scale = lax.rsqrt(head_sums(keys * keys, block) * (1.0 / HEAD) + head_eps)
+        k_unit = keys * k_scale
+        pooled = []
+        for j in range(LATL):
+            e = jnp.exp(head_sums(k_unit * q_unit[j : j + 1], block))
+            top, bottom = 0.0, 0.0
+            for l in range(LEV):
+                part = e[l * WIN : (l + 1) * WIN]
+                top = top + part * vals[l * WIN : (l + 1) * WIN]
+                bottom = bottom + part
+            pooled.append(top / bottom)
+        pooled = jnp.concatenate(pooled, axis=0).astype(BF16)
+        if head:
+            weights[2].wait()
+        latents = mm(pooled, w_pool[...])
+        latents = jnp.concatenate(
+            [latents[j * WIN : (j + 1) * WIN] + query[j : j + 1] for j in range(LATL)], axis=0
+        )
+        return latents.astype(BF16).astype(F32)
+
+
+    def encode_home(c, head):
+        rows = rows32[pl.ds(pl.multiple_of(c * WIN, WIN), WIN), :]
+        latents = encode(split_levels(rows), head)
+        latents = jnp.concatenate([latents[:WIN], latents[WIN:]], axis=1)
+        for i in range(slots_win):
+            block_rows = latents[i * piece_cols : (i + 1) * piece_cols]
+            send_lat[c * slots_win + i] = block_rows.astype(BF16)
+
+    encode_home(0, True)
+    chunks = (n * piece_cols) // WIN
+    if chunks > 1:
+
+        def more_home(c, _):
+            encode_home(c, False)
+            return 0
+
+        lax.fori_loop(1, chunks, more_home, 0)
+
+    pl.semaphore_wait(barrier, n - 1)
+
+    def send_out(source, target_buffer, sent, received):
+        def one(step, _):
+            target = lax.rem(me + step, n)
+            pltpu.make_async_remote_copy(
+                src_ref=source.at[lax.rem(target - my_carry + n, n)],
+                dst_ref=target_buffer.at[my_slot],
+                send_sem=sent,
+                recv_sem=received,
+                device_id={"lon": target},
+                device_id_type=MESH,
+            ).start()
+            return 0
+
+        lax.fori_loop(1, n, one, 0, unroll=unroll)
+        target_buffer[my_slot] = source[lax.rem(me - my_carry + n, n)]
+
+    send_out(send_lat, recv_lat, lat_send_sem, lat_recv_sem)
+    send_out(send, recv, send_sem, recv_sem)
+
+    def all_of(buffer, sem):
+        part = buffer.at[pl.ds(0, n - 1)]
+        return pltpu.make_async_copy(part, part, sem)
+
+    weights[7].wait()
+    w_dec_t[:, :PIN] = w_dec[...].T
+
+    all_of(recv_lat, lat_recv_sem).wait()
+
+    lane = lax.broadcasted_iota(jnp.int32, (WIN, LEV * PAD), 1)
+
+    def window(w, first):
+        for i in range(slots_win):
+            part = recv_lat[w * slots_win + i].astype(F32)
+            work[i * piece_cols : (i + 1) * piece_cols, : LATL * D] = part
+        arrived = work[:, : LATL * D]
         shape = (LATL * WIN, HALF)
         token = lax.rem(lax.broadcasted_iota(jnp.int32, shape, 0), WIN)
         other = lax.rem(lax.broadcasted_iota(jnp.int32, shape, 1), WIN)
@@ -187,35 +244,10 @@
 
         for step in range(STEPS):
             head = first and step == 0
-            tokens = mm(current, w_embed[...])
-            tokens = jnp.concatenate(
-                [tokens[l * WIN : (l + 1) * WIN] + embeds[l] for l in range(LEV)], axis=0
-            )
-            tokens = layer_norm(tokens, enc_gain_ref[...]).astype(BF16)
-            if head:
-                weights[1].wait()
-            keyval = mm(tokens, w_kv[...])
-            keys, vals = keyval[:, :D], keyval[:, D:]
-            k_scale = lax.rsqrt(head_sums(keys * keys, block) * (1.0 / HEAD) + head_eps)
-            k_unit = keys * k_scale
-            pooled = []
-            for j in range(LATL):
-                e = jnp.exp(head_sums(k_unit * q_unit[j : j + 1], block))
-                top, bottom = 0.0, 0.0
-                for l in range(LEV):
-                    part = e[l * WIN : (l + 1) * WIN]
-                    top = top + part * vals[l * WIN : (l + 1) * WIN]
-                    bottom = bottom + part
-                pooled.append(top / bottom)
-            pooled = jnp.concatenate(pooled, axis=0).astype(BF16)
-            if head:
-                weights[2].wait()
-            latents = mm(pooled, w_pool[...])
-            latents = jnp.concatenate(
-                [latents[j * WIN : (j + 1) * WIN] + query[j : j + 1] for j in range(LATL)], axis=0
-            )
-            latents = latents.astype(BF16).astype(F32)
-
+            if step == 0:
+                latents = jnp.concatenate([arrived[:, :D], arrived[:, D:]], axis=0)
+            else:
+                latents = encode(current, False)
             normed = layer_norm(latents, attn_gain_ref[...]).astype(BF16)
             if head:
                 weights[3].wait()
@@ -257,11 +289,14 @@
                 axis=0,
             )
             decoded = layer_norm(blended, dec_gain_ref[...]).astype(BF16)
-            if head:
-                weights[7].wait()
-            added = lax.dot_general(
-                decoded, w_dec[...], (((1,), (1,)), ((), ())), preferred_element_type=F32
-            ).astype(BF16)
+            added = mm(decoded, w_dec_t[:, :PIN]).astype(BF16)
+            if step == 0:
+                if first:
+                    all_of(recv, recv_sem).wait()
+                for i in range(slots_win):
+                    part = recv[w * slots_win + i].astype(F32)
+                    work[i * piece_cols : (i + 1) * piece_cols, :] = part
+                current = split_levels(work[...])
             current = (current.astype(F32) + added.astype(F32)).astype(BF16)
 
         final = current.astype(F32)
@@ -275,7 +310,7 @@
         work[...] = merged
         for i in range(slots_win):
             send_back[w * slots_win + i] = work[
-                i * piece_cols : (i + 1) * piece_cols, :wide
+                i * piece_cols : (i + 1) * piece_cols, :
             ].astype(BF16)
 
     window(0, True)
@@ -304,11 +339,12 @@
     lax.fori_loop(1, n, start_back, 0, unroll=unroll)
     recv_back[lax.rem(me - my_carry + n, n)] = send_back[my_slot]
     all_of(send, send_sem).wait()
+    all_of(send_lat, lat_send_sem).wait()
     all_of(recv_back, recv_back_sem).wait()
 
     def unpack(i, _):
         rows = [recv_back[i * group + k].astype(F32) for k in range(group)]
-        rows32[pl.ds(pl.multiple_of(i * 8, 8), 8), :wide] = jnp.concatenate(rows, axis=0)
+        rows32[pl.ds(pl.multiple_of(i * 8, 8), 8), :] = jnp.concatenate(rows, axis=0)
         return 0
 
     lax.fori_loop(0, n // group, unpack, 0, unroll=unroll)
@@ -337,7 +373,6 @@
     dec_weight,
 ):
     local_count = fields.shape[1]
-    wide = fields.shape[2]
     piece_cols = local_count // n
     lat_count = n // ROW_PARTS
     operands = (
@@ -372,10 +407,15 @@
         + [
             pltpu.VMEM((local_count, LEV * PAD), F32),
             pltpu.VMEM((WIN, LEV * PAD), F32),
-            pltpu.VMEM((n, piece_cols, wide), BF16),
-            pltpu.VMEM((n, piece_cols, wide), BF16),
-            pltpu.VMEM((n, piece_cols, wide), BF16),
-            pltpu.VMEM((n, piece_cols, wide), BF16),
+            pltpu.VMEM((n, piece_cols, LEV * PAD), BF16),
+            pltpu.VMEM((n, piece_cols, LEV * PAD), BF16),
+            pltpu.VMEM((n, piece_cols, LEV * PAD), BF16),
+            pltpu.VMEM((n, piece_cols, LEV * PAD), BF16),
+            pltpu.VMEM((D, PAD), BF16),
+            pltpu.VMEM((n, piece_cols, LATL * D), BF16),
+            pltpu.VMEM((n, piece_cols, LATL * D), BF16),
+            pltpu.SemaphoreType.DMA,
+            pltpu.SemaphoreType.DMA,
             pltpu.SemaphoreType.DMA((len(operands),)),
             pltpu.SemaphoreType.DMA,
             pltpu.SemaphoreType.DMA,

time: 23.9 us -> 22.5 us (0.941)
  Pallas kernels: 23.1 us -> 21.7 us
    pallas_call x1, Pallas kernels: 23.1 us -> 21.7 us  [shards(): pl.pallas_call(functools.partial(kernel, n, lat_count, piece_cols), name=...]
where the time goes in v3:
time: 22.5 us; the launch traced here: 22.4 us
  Pallas kernels  21.7 us (96%)
  local copies, waits for them, and re-layouts  0.64 us (3%)
    pallas_call x1, Pallas kernels, shards(): pl.pallas_call(functools.partial(kernel, n, lat_count, piece_cols), name=...  21.7 us
    unnamed x1, local copies, waits for them, and re-layouts  0.64 us

profile of v3, /device:TPU:0, one launch (start us, length us, event | category | flops | bytes accessed | tf_op | source)
XLA Modules:
  0.0 22.4 jit_solution(13625300048052604638)
XLA Ops:
  0.0 21.7 %forecast.1 = bf16[1,32,1500]{2,1,0:T(8,128)(2,1)S(1)} custom-call(bf16[1,32,1500]{2,1,0:T(8,128)(2,1)} %refs_0_.1, s32[3]{0:T(128)} %refs_1_.1, f32[2,3]{1,0:T(2,128)} %bitcast.11, bf16[3,512]{1,0:T(4,128)(2,1)} %refs_3_.1, bf16[2,512]{1,0:T(2,128)(2,1)} %refs_4_.1, f32[1,512]{1,0:T(1,128)} %bitcast.7, f32[1,512]{1,0:T(1,128)} %bitcast.8, ...), custom_call_target="tpu_custom_call" | custom-call | tf_op jit(solution)/shard_map/forecast/pallas_call | solution.py:398
  21.7 0.6 %copy.19 = bf16[1,32,1500]{2,1,0:T(8,128)(2,1)} copy(bf16[1,32,1500]{2,1,0:T(8,128)(2,1)S(1)} %forecast.1) | data formatting | bytes 192000
